TPU v7x, 256 devices: a whole 4x4x8 slice. The times are simulated.
256 devices in a mesh: row: 32 (over z, x_hi, core), col: 8 (over y, x_lo).
Axes of the slice: x: 4 (x_hi: 2, x_lo: 2; x = x_hi * 2 + x_lo), y: 4, z: 8, core: 2. Of those that a mesh axis runs over, the one named last changes fastest.
Arguments:
- object_field: float32 [2, 2, 4096, 1024], P(None, None, 'row', 'col'), may hold values from -1 to 1
- probe: float32 [4, 2, 128, 128], replicated, may hold values from -3 to 3
- kernel_phase: float32 [128, 128], replicated, may hold values from -3.140625 to 3.140625
- amplitudes: float32 [3, 32, 8, 128, 128], P(None, 'row', 'col'), may hold values from 0.05 to 1
- offsets: int32 [3, 32, 8, 2], P(None, 'row', 'col'), may hold values from 0 to 64
Outputs:
- object_out: float32 [2, 2, 4096, 1024], P(None, None, 'row', 'col')
- probe_out: float32 [4, 2, 128, 128], replicated
Inputs may be any that keep to these rules, and one draw needn't show every extreme that they name: offsets[b, r + p, c] place a window of 128 x 128 pixels inside tile (r, c) extended by 32 pixels on each side.
All inputs are finite; a program needn't handle non-finite values.
Results may differ from a plain program's by a relative error of at most 0.0003.
Values sent between devices are 32-bit elements; how exact they have to be, the bound alone decides.
No kernel may reach another device: no remote copies, remote signals or barrier semaphores. Data moves between devices by JAX's collectives and lax.ppermute only.
A program may use at most 128 MiB of HBM per device.

v0:
```python
import math
import jax
import jax.numpy as jnp
from jax import lax
from jax.sharding import PartitionSpec as P

WIN = 128
OVL = 32
SLICES = 2
OBJECT_RATE = 0.5
PROBE_RATE = 0.5
FLOOR = 0.1
HIGHEST = lax.Precision.HIGHEST


def shifted(block, axis, distance):
    devices = range(lax.axis_size(axis))
    route = [(i - distance, i) for i in devices if i - distance in devices]
    return lax.ppermute(block, axis, route)


def filled_up(lines, count):
    spare = -lines.shape[0] % count
    if not spare:
        return lines
    return jnp.concatenate([lines, jnp.zeros((spare, *lines.shape[1:]), lines.dtype)])


def sum_by_parts(x, axis):
    lines = x.reshape(-1, *x.shape[1:][-1:])
    padded = filled_up(lines, lax.axis_size(axis))
    own = lax.psum_scatter(padded, axis, scatter_dimension=0, tiled=True)
    whole = lax.all_gather(own, axis, axis=0, tiled=True)
    return whole[: len(lines)].reshape(x.shape)


def extended_2(cells, sides, width):
    for axis, dim in sides:
        count = lax.axis_size(axis)
        ends = count - 1
        head = lax.slice_in_dim(cells, 0, width, axis=dim)
        tail = lax.slice_in_dim(cells, cells.shape[dim] - width, cells.shape[dim], axis=dim)
        cells = jnp.concatenate(
            [
                lax.ppermute(tail, axis, [(i, (i + 1) % count) for i in range(ends)]),
                cells,
                lax.ppermute(head, axis, [((i + 1) % count, i) for i in range(ends)]),
            ],
            axis=dim,
        )
    return cells


def dft_tables(window):
    counter = jnp.arange(window, dtype=jnp.int32)
    product = counter[:, None] * counter[None, :] % window
    phases = product.astype(jnp.float32) * (-2.0 * math.pi / window)
    scaling = 1.0 / math.sqrt(window)
    return (jnp.cos(phases) * scaling, jnp.sin(phases) * scaling)


def left_apply(matrix, values):
    return jnp.einsum("ij,bjk->bik", matrix, values, precision=HIGHEST)


def right_apply(values, matrix):
    return jnp.einsum("bij,jk->bik", values, matrix, precision=HIGHEST)


def transform(field_pair, tables, inverse):
    cosine, sine = tables
    if inverse:
        sine = -sine
    real_part, imag_part = field_pair
    shape = real_part.shape
    window = shape[-1]
    real_part = real_part.reshape(-1, window, window)
    imag_part = imag_part.reshape(-1, window, window)
    middle_real = left_apply(cosine, real_part) - left_apply(sine, imag_part)
    middle_imag = left_apply(cosine, imag_part) + left_apply(sine, real_part)
    result_real = right_apply(middle_real, cosine) - right_apply(middle_imag, sine)
    result_imag = right_apply(middle_imag, cosine) + right_apply(middle_real, sine)
    return (result_real.reshape(shape), result_imag.reshape(shape))


def complex_product(left_pair, right_pair):
    left_real, left_imag = left_pair
    right_real, right_imag = right_pair
    return (
        left_real * right_real - left_imag * right_imag,
        left_real * right_imag + left_imag * right_real,
    )


def conj_product(left_pair, right_pair):
    left_real, left_imag = left_pair
    right_real, right_imag = right_pair
    return (
        left_real * right_real + left_imag * right_imag,
        left_real * right_imag - left_imag * right_real,
    )


def propagate(field_pair, kernel, tables, adjoint):
    spectrum = transform(field_pair, tables, False)
    phase_pair = (kernel[0], -kernel[1]) if adjoint else kernel
    return transform(complex_product(spectrum, phase_pair), tables, True)


def window_gradients(windows, probe_now, kernel, measured, tables):
    first_slice = (windows[:, 0, 0][:, None], windows[:, 0, 1][:, None])
    second_slice = (windows[:, 1, 0][:, None], windows[:, 1, 1][:, None])
    probe_wave = (probe_now[None, :, 0], probe_now[None, :, 1])
    entrance = complex_product(probe_wave, first_slice)
    spread = propagate(entrance, kernel, tables, False)
    exit_wave = complex_product(spread, second_slice)
    farfield = transform(exit_wave, tables, False)
    intensity = jnp.sum(
        farfield[0] * farfield[0] + farfield[1] * farfield[1], axis=1, keepdims=True
    )
    factor = 1.0 - measured[:, None] / jnp.sqrt(intensity + FLOOR)
    back_second = transform((farfield[0] * factor, farfield[1] * factor), tables, True)
    second_terms = conj_product(spread, back_second)
    grad_second = (jnp.sum(second_terms[0], axis=1), jnp.sum(second_terms[1], axis=1))
    back_first = propagate(conj_product(second_slice, back_second), kernel, tables, True)
    first_terms = conj_product(probe_wave, back_first)
    grad_first = (jnp.sum(first_terms[0], axis=1), jnp.sum(first_terms[1], axis=1))
    probe_terms = conj_product(first_slice, back_first)
    grad_probe = (jnp.sum(probe_terms[0], axis=0), jnp.sum(probe_terms[1], axis=0))
    object_grad = jnp.stack([jnp.stack(grad_first, axis=1), jnp.stack(grad_second, axis=1)], axis=1)
    probe_grad = jnp.stack(grad_probe, axis=1)
    return (object_grad, probe_grad)


def fold_rows(buffer):
    inner = buffer.shape[2] - 2 * OVL
    upper = buffer[:, :, :OVL]
    lower = buffer[:, :, inner + OVL :]
    from_below = shifted(upper, "row", -1)
    from_above = shifted(lower, "row", 1)
    middle = buffer[:, :, OVL : inner + OVL]
    middle = middle.at[:, :, inner - OVL :].add(from_below)
    middle = middle.at[:, :, :OVL].add(from_above)
    return middle


def fold_cols(buffer):
    inner = buffer.shape[3] - 2 * OVL
    leftmost = buffer[:, :, :, :OVL]
    rightmost = buffer[:, :, :, inner + OVL :]
    from_right = shifted(leftmost, "col", -1)
    from_left = shifted(rightmost, "col", 1)
    middle = buffer[:, :, :, OVL : inner + OVL]
    middle = middle.at[:, :, :, inner - OVL :].add(from_right)
    middle = middle.at[:, :, :, :OVL].add(from_left)
    return middle


def probe_total(local_grad):
    partial_sum = sum_by_parts(local_grad, "row")
    return sum_by_parts(partial_sum, "col")


def per_device(object_field, probe, kernel_phase, amplitudes, offsets):
    tables = dft_tables(probe.shape[-1])
    kernel = (jnp.cos(kernel_phase), jnp.sin(kernel_phase))
    devices = lax.axis_size("row") * lax.axis_size("col")
    positions = offsets.shape[1]
    batch_count = offsets.shape[0]
    probe_rate = PROBE_RATE / math.sqrt(devices * positions)
    anchor = jnp.zeros((), jnp.int32)
    window_shape = (SLICES, 2, WIN, WIN)
    current = object_field
    probe_now = probe
    pending = None
    held = None
    for batch_index in range(batch_count):
        extended = extended_2(current, (("row", 2), ("col", 3)), OVL)
        position = 0
        starts = (
            anchor,
            anchor,
            offsets[batch_index, position, 0, 0],
            offsets[batch_index, position, 0, 1],
        )
        start_list = [starts]
        window_list = [lax.dynamic_slice(extended, starts, window_shape)]
        windows = jnp.stack(window_list)
        object_grad, probe_grad = window_gradients(
            windows, probe_now, kernel, amplitudes[batch_index, :, 0], tables
        )
        accumulated = jnp.zeros_like(extended)
        position = 0
        accumulated = lax.dynamic_update_slice(
            accumulated, object_grad[position], start_list[position]
        )
        folded = fold_cols(fold_rows(accumulated))
        current = current - OBJECT_RATE * folded
        if batch_index >= batch_count - 2:
            held = probe_grad if held is None else held + probe_grad
            summed = None
        else:
            summed = probe_total(probe_grad)
        if pending is not None:
            probe_now = probe_now - probe_rate * pending
        pending = summed
    probe_now = probe_now - probe_rate * probe_total(held)
    return (current, probe_now)


def solution(mesh):
    in_specs = (
        P(None, None, "row", "col"),
        P(),
        P(),
        P(None, "row", "col", None, None),
        P(None, "row", "col", None),
    )
    out_specs = (P(None, None, "row", "col"), P())
    return jax.shard_map(
        per_device, mesh=mesh, in_specs=in_specs, out_specs=out_specs, check_vma=False
    )
```

profile of v0, /device:TPU:4, one launch (start us, length us, event | category | flops | bytes accessed | tf_op | source)
XLA Modules:
  0.0 705.8 jit_solution(17390256663919883016)
XLA Ops:
  10.1 5.1 collective-permute-start.1
  17.3 3.1 collective-permute-start.2
  27.1 11.6 %collective-permute-done.3 = f32[2,2,192,32]{3,2,1,0:T(8,128)S(1)} collective-permute-done((f32[2,2,192,32]{3,2,1,0:T(8,128)S(1)}, f32[2,2,192,32]{3,2,1,0:T(8,128)S(1)}, u32[]{:S(2)}, u32[]{:S(2)}) %collective-permute-start.3) | collective-permute-done | bytes 98336 | tf_op jit(solution)/shard_map/ppermute | solution.py:47
  77.2 3.1 dynamic_update_slice.9
  80.3 2.5 collective-permute-start.4
  82.9 3.1 collective-permute-start.5
  86.0 6.1 collective-permute-done.5
  93.7 4.7 collective-permute-start.7
  98.4 5.1 collective-permute-done.6
  107.3 5.1 collective-permute-start.9
  115.3 4.8 collective-permute-start.10
  126.2 12.7 %collective-permute-done.11 = f32[2,2,192,32]{3,2,1,0:T(8,128)S(1)} collective-permute-done((f32[2,2,192,32]{3,2,1,0:T(8,128)S(1)}, f32[2,2,192,32]{3,2,1,0:T(8,128)S(1)}, u32[]{:S(2)}, u32[]{:S(2)}) %collective-permute-start.11) | collective-permute-done | bytes 98336 | tf_op jit(solution)/shard_map/ppermute | solution.py:47
  177.6 3.1 dynamic_update_slice.10
  180.8 3.6 collective-permute-start.12
  184.4 3.0 collective-permute-start.13
  187.5 6.1 collective-permute-done.13
  196.9 4.6 collective-permute-start.15
  201.4 3.5 collective-permute-done.14
  207.6 110.5 %reduce-scatter.5.cloned.1.call-done = f32[32,128]{1,0:T(8,128)} async-done(((f32[1024,128]{1,0:T(8,128)}), f32[32,128]{1,0:T(8,128)}) %reduce-scatter.5.cloned.1.call-update) | async-done | bytes 16400 | tf_op jit(solution)/shard_map/reduce_scatter | solution.py:32
  318.1 42.3 %all_gather.12 = f32[1024,128]{1,0:T(8,128)} all-gather(f32[32,128]{1,0:T(8,128)} %reduce-scatter.5.cloned.1.call-done), channel_id=1, replica_groups=mesh['row'=32,'col'=8] {'row'}, dimensions={0}, use_global_device_ids=true | all-gather | bytes 540672 | tf_op jit(solution)/shard_map/all_gather | solution.py:33
  362.7 4.8 collective-permute-start.17
  369.6 3.1 collective-permute-start.18
  377.6 6.3 collective-permute-done.18
  383.9 16.4 %collective-permute-done.19 = f32[2,2,192,32]{3,2,1,0:T(8,128)S(1)} collective-permute-done((f32[2,2,192,32]{3,2,1,0:T(8,128)S(1)}, f32[2,2,192,32]{3,2,1,0:T(8,128)S(1)}, u32[]{:S(2)}, u32[]{:S(2)}) %collective-permute-start.19) | collective-permute-done | bytes 98336 | tf_op jit(solution)/shard_map/ppermute | solution.py:47
  403.1 30.0 %all_gather.13 = f32[1024,128]{1,0:T(8,128)S(1)} all-gather(f32[128,128]{1,0:T(8,128)} %reduce-scatter.7.cloned.1.call-done), channel_id=1, replica_groups=mesh['row'=32,'col'=8] {'col'}, dimensions={0}, use_global_device_ids=true | all-gather | bytes 589824 | tf_op jit(solution)/shard_map/all_gather | solution.py:33
  472.1 3.1 dynamic_update_slice.11
  479.8 104.7 %reduce-scatter.9.cloned.1.call-done = f32[32,128]{1,0:T(8,128)} async-done(((f32[1024,128]{1,0:T(8,128)}), f32[32,128]{1,0:T(8,128)}) %reduce-scatter.9.cloned.1.call-update) | async-done | bytes 16400 | tf_op jit(solution)/shard_map/reduce_scatter | solution.py:32
  584.5 42.4 %all_gather.14 = f32[1024,128]{1,0:T(8,128)} all-gather(f32[32,128]{1,0:T(8,128)} %reduce-scatter.9.cloned.1.call-done), channel_id=1, replica_groups=mesh['row'=32,'col'=8] {'row'}, dimensions={0}, use_global_device_ids=true | all-gather | bytes 540672 | tf_op jit(solution)/shard_map/all_gather | solution.py:33
  628.5 4.6 collective-permute-start.23
  633.1 5.1 collective-permute-done.22
  641.5 26.1 %reduce-scatter.11.cloned.1.call-done = f32[128,128]{1,0:T(8,128)} async-done(((f32[1024,128]{1,0:T(8,128)}), f32[128,128]{1,0:T(8,128)}) %reduce-scatter.11.cloned.1.call-update) | async-done | bytes 65552 | tf_op jit(solution)/shard_map/reduce_scatter | solution.py:32
  667.6 30.3 %all_gather.15 = f32[1024,128]{1,0:T(8,128)S(1)} all-gather(f32[128,128]{1,0:T(8,128)} %reduce-scatter.11.cloned.1.call-done), channel_id=1, replica_groups=mesh['row'=32,'col'=8] {'col'}, dimensions={0}, use_global_device_ids=true | all-gather | bytes 589824 | tf_op jit(solution)/shard_map/all_gather | solution.py:33
  (265 shorter events, 158.0 us)
Async XLA Ops:
  7.2 9.2 %copy-start.1 = (f32[2,2,128,128]{3,2,1,0:T(8,128)S(1)}, f32[2,2,128,128]{3,2,1,0:T(8,128)}, u32[]{:S(2)}) copy-start(f32[2,2,128,128]{3,2,1,0:T(8,128)} %param.29) | copy-start | bytes 786436
  7.2 310.9 %reduce-scatter.5.cloned.1.call-start = ((), (), s32[]{:S(2)}) async-start(), calls=%async_computation.4 | async-start | bytes 540672 | tf_op jit(solution)/shard_map/reduce_scatter | solution.py:32
  8.1 8.2 %collective-permute-start = (f32[2,2,32,128]{3,2,1,0:T(8,128)S(1)}, f32[2,2,32,128]{3,2,1,0:T(8,128)S(1)}, u32[]{:S(2)}, u32[]{:S(2)}) collective-permute-start(f32[2,2,32,128]{3,2,1,0:T(8,128)S(1)} %get-tuple-element.209), channel_id=1, source_target_pairs={{0,8},{8,16},{16,24},{24,32},{32,40},{40,48},{48,56},{56,64},{64,7... | collective-permute-start | bytes 196616 | tf_op jit(solution)/shard_map/ppermute | solution.py:45
  10.1 7.0 collective-permute-start.1
  17.3 4.4 copy-start.4
  17.3 9.8 %collective-permute-start.2 = (f32[2,2,192,32]{3,2,1,0:T(8,128)S(1)}, f32[2,2,192,32]{3,2,1,0:T(8,128)S(1)}, u32[]{:S(2)}, u32[]{:S(2)}) collective-permute-start(f32[2,2,192,32]{3,2,1,0:T(8,128)S(1)} %get-tuple-element.191), channel_id=1, source_target_pairs={{0,1},{1,2},{2,3},{3,4},{4,5},{5,6},{6,7},{8,9},{9,10},{10,11},{11... | collective-permute-start | bytes 294920 | tf_op jit(solution)/shard_map/ppermute | solution.py:45
  20.4 18.2 %collective-permute-start.3 = (f32[2,2,192,32]{3,2,1,0:T(8,128)S(1)}, f32[2,2,192,32]{3,2,1,0:T(8,128)S(1)}, u32[]{:S(2)}, u32[]{:S(2)}) collective-permute-start(f32[2,2,192,32]{3,2,1,0:T(8,128)S(1)} %get-tuple-element.190), channel_id=1, source_target_pairs={{1,0},{2,1},{3,2},{4,3},{5,4},{6,5},{7,6},{9,8},{10,9},{11,10},{12... | collective-permute-start | bytes 294920 | tf_op jit(solution)/shard_map/ppermute | solution.py:47
  39.0 1.0 copy-start
  80.3 5.6 collective-permute-start.4
  82.9 9.2 %collective-permute-start.5 = (f32[2,2,32,192]{3,2,1,0:T(8,128)S(1)}, f32[2,2,32,192]{3,2,1,0:T(8,128)S(1)}, u32[]{:S(2)}, u32[]{:S(2)}) collective-permute-start(f32[2,2,32,192]{3,2,1,0:T(8,128)S(1)} %get-tuple-element.166), channel_id=1, source_target_pairs={{0,8},{8,16},{16,24},{24,32},{32,40},{40,48},{48,56},{56,64},{64,7... | collective-permute-start | bytes 294920 | tf_op jit(solution)/shard_map/ppermute | solution.py:19
  92.3 11.2 %collective-permute-start.6 = (f32[2,2,128,32]{3,2,1,0:T(8,128)S(1)}, f32[2,2,128,32]{3,2,1,0:T(8,128)S(1)}, u32[]{:S(2)}, u32[]{:S(2)}) collective-permute-start(f32[2,2,128,32]{3,2,1,0:T(8,128)S(1)} %get-tuple-element.185), channel_id=1, source_target_pairs={{1,0},{2,1},{3,2},{4,3},{5,4},{6,5},{7,6},{9,8},{10,9},{11,10},{12... | collective-permute-start | bytes 196616 | tf_op jit(solution)/shard_map/ppermute | solution.py:19
  93.7 11.0 %collective-permute-start.7 = (f32[2,2,128,32]{3,2,1,0:T(8,128)S(1)}, f32[2,2,128,32]{3,2,1,0:T(8,128)S(1)}, u32[]{:S(2)}, u32[]{:S(2)}) collective-permute-start(f32[2,2,128,32]{3,2,1,0:T(8,128)S(1)} %get-tuple-element.184), channel_id=1, source_target_pairs={{0,1},{1,2},{2,3},{3,4},{4,5},{5,6},{6,7},{8,9},{9,10},{10,11},{11... | collective-permute-start | bytes 196616 | tf_op jit(solution)/shard_map/ppermute | solution.py:19
  105.4 7.1 %collective-permute-start.8 = (f32[2,2,32,128]{3,2,1,0:T(8,128)S(1)}, f32[2,2,32,128]{3,2,1,0:T(8,128)S(1)}, u32[]{:S(2)}, u32[]{:S(2)}) collective-permute-start(f32[2,2,32,128]{3,2,1,0:T(8,128)S(1)} %get-tuple-element.202), channel_id=1, source_target_pairs={{0,8},{8,16},{16,24},{24,32},{32,40},{40,48},{48,56},{56,64},{64,7... | collective-permute-start | bytes 196616 | tf_op jit(solution)/shard_map/ppermute | solution.py:45
  107.3 7.0 collective-permute-start.9
  115.3 10.9 %collective-permute-start.10 = (f32[2,2,192,32]{3,2,1,0:T(8,128)}, f32[2,2,192,32]{3,2,1,0:T(8,128)S(1)}, u32[]{:S(2)}, u32[]{:S(2)}) collective-permute-start(f32[2,2,192,32]{3,2,1,0:T(8,128)} %get-tuple-element.189), channel_id=1, source_target_pairs={{0,1},{1,2},{2,3},{3,4},{4,5},{5,6},{6,7},{8,9},{9,10},{10,11},{11... | collective-permute-start | bytes 294920 | tf_op jit(solution)/shard_map/ppermute | solution.py:45
  120.1 18.8 %collective-permute-start.11 = (f32[2,2,192,32]{3,2,1,0:T(8,128)S(1)}, f32[2,2,192,32]{3,2,1,0:T(8,128)S(1)}, u32[]{:S(2)}, u32[]{:S(2)}) collective-permute-start(f32[2,2,192,32]{3,2,1,0:T(8,128)S(1)} %get-tuple-element.188), channel_id=1, source_target_pairs={{1,0},{2,1},{3,2},{4,3},{5,4},{6,5},{7,6},{9,8},{10,9},{11,10},{12... | collective-permute-start | bytes 294920 | tf_op jit(solution)/shard_map/ppermute | solution.py:47
  180.8 6.6 collective-permute-start.12
  184.4 9.2 %collective-permute-start.13 = (f32[2,2,32,192]{3,2,1,0:T(8,128)S(1)}, f32[2,2,32,192]{3,2,1,0:T(8,128)S(1)}, u32[]{:S(2)}, u32[]{:S(2)}) collective-permute-start(f32[2,2,32,192]{3,2,1,0:T(8,128)S(1)} %get-tuple-element.164), channel_id=1, source_target_pairs={{0,8},{8,16},{16,24},{24,32},{32,40},{40,48},{48,56},{56,64},{64,7... | collective-permute-start | bytes 294920 | tf_op jit(solution)/shard_map/ppermute | solution.py:19
  194.5 10.5 %collective-permute-start.14 = (f32[2,2,128,32]{3,2,1,0:T(8,128)S(1)}, f32[2,2,128,32]{3,2,1,0:T(8,128)S(1)}, u32[]{:S(2)}, u32[]{:S(2)}) collective-permute-start(f32[2,2,128,32]{3,2,1,0:T(8,128)S(1)} %get-tuple-element.183), channel_id=1, source_target_pairs={{1,0},{2,1},{3,2},{4,3},{5,4},{6,5},{7,6},{9,8},{10,9},{11,10},{12... | collective-permute-start | bytes 196616 | tf_op jit(solution)/shard_map/ppermute | solution.py:19
  196.7 206.4 %reduce-scatter.7.cloned.1.call-start = ((), (), s32[]{:S(2)}) async-start(), calls=%async_computation.5 | async-start | bytes 589824 | tf_op jit(solution)/shard_map/reduce_scatter | solution.py:32
  196.9 10.2 %collective-permute-start.15 = (f32[2,2,128,32]{3,2,1,0:T(8,128)}, f32[2,2,128,32]{3,2,1,0:T(8,128)S(1)}, u32[]{:S(2)}, u32[]{:S(2)}) collective-permute-start(f32[2,2,128,32]{3,2,1,0:T(8,128)} %get-tuple-element.182), channel_id=1, source_target_pairs={{0,1},{1,2},{2,3},{3,4},{4,5},{5,6},{6,7},{8,9},{9,10},{10,11},{11... | collective-permute-start | bytes 196616 | tf_op jit(solution)/shard_map/ppermute | solution.py:19
  360.4 224.1 %reduce-scatter.9.cloned.1.call-start = ((), (), s32[]{:S(2)}) async-start(), calls=%async_computation.6 | async-start | bytes 540672 | tf_op jit(solution)/shard_map/reduce_scatter | solution.py:32
  360.5 7.1 %collective-permute-start.16 = (f32[2,2,32,128]{3,2,1,0:T(8,128)S(1)}, f32[2,2,32,128]{3,2,1,0:T(8,128)S(1)}, u32[]{:S(2)}, u32[]{:S(2)}) collective-permute-start(f32[2,2,32,128]{3,2,1,0:T(8,128)S(1)} %get-tuple-element.196), channel_id=1, source_target_pairs={{0,8},{8,16},{16,24},{24,32},{32,40},{40,48},{48,56},{56,64},{64,7... | collective-permute-start | bytes 196616 | tf_op jit(solution)/shard_map/ppermute | solution.py:45
  362.7 6.7 collective-permute-start.17
  369.6 14.2 %collective-permute-start.18 = (f32[2,2,192,32]{3,2,1,0:T(8,128)S(1)}, f32[2,2,192,32]{3,2,1,0:T(8,128)S(1)}, u32[]{:S(2)}, u32[]{:S(2)}) collective-permute-start(f32[2,2,192,32]{3,2,1,0:T(8,128)S(1)} %get-tuple-element.187), channel_id=1, source_target_pairs={{0,1},{1,2},{2,3},{3,4},{4,5},{5,6},{6,7},{8,9},{9,10},{10,11},{11... | collective-permute-start | bytes 294920 | tf_op jit(solution)/shard_map/ppermute | solution.py:45
  372.8 27.5 %collective-permute-start.19 = (f32[2,2,192,32]{3,2,1,0:T(8,128)S(1)}, f32[2,2,192,32]{3,2,1,0:T(8,128)S(1)}, u32[]{:S(2)}, u32[]{:S(2)}) collective-permute-start(f32[2,2,192,32]{3,2,1,0:T(8,128)S(1)} %get-tuple-element.186), channel_id=1, source_target_pairs={{1,0},{2,1},{3,2},{4,3},{5,4},{6,5},{7,6},{9,8},{10,9},{11,10},{12... | collective-permute-start | bytes 294920 | tf_op jit(solution)/shard_map/ppermute | solution.py:47
  470.1 1.0 copy-start.2
  471.9 195.7 %reduce-scatter.11.cloned.1.call-start = ((), (), s32[]{:S(2)}) async-start(), calls=%async_computation.7 | async-start | bytes 589824 | tf_op jit(solution)/shard_map/reduce_scatter | solution.py:32
  475.3 4.4 collective-permute-start.20
  477.3 149.6 %collective-permute-start.21 = (f32[2,2,32,192]{3,2,1,0:T(8,128)S(1)}, f32[2,2,32,192]{3,2,1,0:T(8,128)S(1)}, u32[]{:S(2)}, u32[]{:S(2)}) collective-permute-start(f32[2,2,32,192]{3,2,1,0:T(8,128)S(1)} %get-tuple-element.162), channel_id=1, source_target_pairs={{0,8},{8,16},{16,24},{24,32},{32,40},{40,48},{48,56},{56,64},{64,7... | collective-permute-start | bytes 294920 | tf_op jit(solution)/shard_map/ppermute | solution.py:19
  627.1 11.1 %collective-permute-start.22 = (f32[2,2,128,32]{3,2,1,0:T(8,128)S(1)}, f32[2,2,128,32]{3,2,1,0:T(8,128)S(1)}, u32[]{:S(2)}, u32[]{:S(2)}) collective-permute-start(f32[2,2,128,32]{3,2,1,0:T(8,128)S(1)} %get-tuple-element.179), channel_id=1, source_target_pairs={{1,0},{2,1},{3,2},{4,3},{5,4},{6,5},{7,6},{9,8},{10,9},{11,10},{12... | collective-permute-start | bytes 196616 | tf_op jit(solution)/shard_map/ppermute | solution.py:19
  628.5 11.8 %collective-permute-start.23 = (f32[2,2,128,32]{3,2,1,0:T(8,128)S(1)}, f32[2,2,128,32]{3,2,1,0:T(8,128)S(1)}, u32[]{:S(2)}, u32[]{:S(2)}) collective-permute-start(f32[2,2,128,32]{3,2,1,0:T(8,128)S(1)} %get-tuple-element.178), channel_id=1, source_target_pairs={{0,1},{1,2},{2,3},{3,4},{4,5},{5,6},{6,7},{8,9},{9,10},{10,11},{11... | collective-permute-start | bytes 196616 | tf_op jit(solution)/shard_map/ppermute | solution.py:19
  (1 other events, 0.9 us)
Sparse Core Ops, SparseCore 0:
  196.8 121.2 reduce-scatter.4
  360.5 42.5 reduce-scatter.6
  472.1 112.3 reduce-scatter.8
  627.0 40.5 reduce-scatter.10
where the time goes:
time: 716 us; the launch traced here: 706 us
  waiting for transfers between devices  325 us (45%)
  blocking collectives  145 us (20%)
  matrix products  111 us (16%)
  starting transfers between devices  70.5 us (10%)
  between operations  27.1 us (4%)
  local copies, waits for them, and re-layouts  24.3 us (3%)
    reduce_scatter x4, waiting for transfers between devices, sum_by_parts(): own = lax.psum_scatter(padded, axis, scatter_dimension=0, tiled=True)  244 us
    all_gather x4, blocking collectives, sum_by_parts(): whole = lax.all_gather(own, axis, axis=0, tiled=True)  145 us
    dot_general x72, matrix products, right_apply(): return jnp.einsum('bij,jk->bik', values, matrix, precision=HIGHEST)  55.8 us
    dot_general x72, matrix products, left_apply(): return jnp.einsum('ij,bjk->bik', matrix, values, precision=HIGHEST)  55.1 us
    ppermute x6, waiting for transfers between devices, extended_2(): lax.ppermute(head, axis, [((i + 1) % count, i) for i in range(ends)])  45.2 us
    ppermute x12, starting transfers between devices, shifted(): return lax.ppermute(block, axis, route)  34.2 us
    ppermute x12, waiting for transfers between devices, shifted(): return lax.ppermute(block, axis, route)  27.6 us
    ppermute x6, starting transfers between devices, extended_2(): lax.ppermute(head, axis, [((i + 1) % count, i) for i in range(ends)])  19 us
  transfers between devices with their start and end apart: 28, of which 20 were waited for; matrix products, arithmetic and copies ran while one was open for 2% of the time, Pallas kernels for 0%

commit v1 on v0

--- a/solution.py
+++ b/solution.py
@@ -30,7 +30,8 @@
     lines = x.reshape(-1, *x.shape[1:][-1:])
     padded = filled_up(lines, lax.axis_size(axis))
     own = lax.psum_scatter(padded, axis, scatter_dimension=0, tiled=True)
-    whole = lax.all_gather(own, axis, axis=0, tiled=True)
+    stack = jnp.stack([own] * lax.axis_size(axis))
+    whole = jnp.concatenate(lax.all_to_all(stack, axis, 0, 0), axis=0)
     return whole[: len(lines)].reshape(x.shape)
 
 

time: 716 us -> 601 us (0.84)
  blocking collectives: 145 us -> 0 us
  starting transfers between devices: 70.5 us -> 91.6 us
  local copies, waits for them, and re-layouts: 24.3 us -> 32.9 us
    all_gather x4 -> x0, blocking collectives: 145 us -> none  [sum_by_parts(): whole = lax.all_gather(own, axis, axis=0, tiled=True)]
    reduce_scatter x4, waiting for transfers between devices: 244 us -> 221 us  [sum_by_parts(): own = lax.psum_scatter(padded, axis, scatter_dimension=0, tiled=True)]
    all_to_all x0 -> x4, starting transfers between devices: none -> 22 us  [sum_by_parts(): whole = jnp.concatenate(lax.all_to_all(stack, axis, 0, 0), axis=0)]
    all_to_all x0 -> x4, waiting for transfers between devices: none -> 19.7 us  [sum_by_parts(): whole = jnp.concatenate(lax.all_to_all(stack, axis, 0, 0), axis=0)]
  transfers between devices with their start and end apart: 28 -> 32, of which waited for: 20 -> 22; matrix products, arithmetic and copies ran while one was open for 2% -> 10% of each run, Pallas kernels for 0% -> 0%
where the time goes in v1:
time: 601 us; the launch traced here: 590 us
  waiting for transfers between devices  323 us (54%)
  matrix products  111 us (18%)
  starting transfers between devices  91.6 us (15%)
  local copies, waits for them, and re-layouts  32.9 us (5%)
  between operations  27.1 us (5%)
    reduce_scatter x4, waiting for transfers between devices, sum_by_parts(): own = lax.psum_scatter(padded, axis, scatter_dimension=0, tiled=True)  221 us
    dot_general x72, matrix products, right_apply(): return jnp.einsum('bij,jk->bik', values, matrix, precision=HIGHEST)  55.8 us
    dot_general x72, matrix products, left_apply(): return jnp.einsum('ij,bjk->bik', matrix, values, precision=HIGHEST)  55 us
    ppermute x6, waiting for transfers between devices, extended_2(): lax.ppermute(head, axis, [((i + 1) % count, i) for i in range(ends)])  39.3 us
    ppermute x12, waiting for transfers between devices, shifted(): return lax.ppermute(block, axis, route)  34.1 us
    ppermute x12, starting transfers between devices, shifted(): return lax.ppermute(block, axis, route)  32.6 us
    all_to_all x4, starting transfers between devices, sum_by_parts(): whole = jnp.concatenate(lax.all_to_all(stack, axis, 0, 0), axis=0)  22 us
    ppermute x6, starting transfers between devices, extended_2(): lax.ppermute(tail, axis, [(i, (i + 1) % count) for i in range(ends)])  20.5 us
  transfers between devices with their start and end apart: 32, of which 22 were waited for; matrix products, arithmetic and copies ran while one was open for 10% of the time, Pallas kernels for 0%

profile of v1, /device:TPU:4, one launch (start us, length us, event | category | flops | bytes accessed | tf_op | source)
XLA Modules:
  0.0 590.1 jit_solution(2099590124276406625)
XLA Ops:
  10.1 5.1 collective-permute-start.1
  17.3 3.1 collective-permute-start.2
  27.1 11.6 %collective-permute-done.3 = f32[2,2,192,32]{3,2,1,0:T(8,128)S(1)} collective-permute-done((f32[2,2,192,32]{3,2,1,0:T(8,128)S(1)}, f32[2,2,192,32]{3,2,1,0:T(8,128)S(1)}, u32[]{:S(2)}, u32[]{:S(2)}) %collective-permute-start.3) | collective-permute-done | bytes 98336 | tf_op jit(solution)/shard_map/ppermute | solution.py:48
  77.9 3.1 dynamic_update_slice.9
  86.8 6.1 %collective-permute-done.5 = f32[2,2,32,192]{3,2,1,0:T(8,128)S(1)} collective-permute-done((f32[2,2,32,192]{3,2,1,0:T(8,128)S(1)}, f32[2,2,32,192]{3,2,1,0:T(8,128)S(1)}, u32[]{:S(2)}, u32[]{:S(2)}) %collective-permute-start.5) | collective-permute-done | bytes 98336 | tf_op jit(solution)/shard_map/ppermute | solution.py:19
  94.5 4.7 collective-permute-start.7
  99.1 5.1 collective-permute-done.6
  108.0 5.1 collective-permute-start.9
  118.0 4.8 collective-permute-start.10
  125.1 5.9 collective-permute-done.10
  131.0 12.7 %collective-permute-done.11 = f32[2,2,192,32]{3,2,1,0:T(8,128)S(1)} collective-permute-done((f32[2,2,192,32]{3,2,1,0:T(8,128)S(1)}, f32[2,2,192,32]{3,2,1,0:T(8,128)S(1)}, u32[]{:S(2)}, u32[]{:S(2)}) %collective-permute-start.11) | collective-permute-done | bytes 98336 | tf_op jit(solution)/shard_map/ppermute | solution.py:48
  183.1 3.1 dynamic_update_slice.10
  186.2 60.4 %reduce-scatter.5.cloned.1.call-done = f32[32,128]{1,0:T(8,128)} async-done(((f32[1024,128]{1,0:T(8,128)}), f32[32,128]{1,0:T(8,128)}) %reduce-scatter.5.cloned.1.call-update) | async-done | bytes 16400 | tf_op jit(solution)/shard_map/reduce_scatter | solution.py:32
  248.2 7.5 %all-to-all-start = ((f32[32,32,128]{2,1,0:T(8,128)}), f32[32,32,128]{2,1,0:T(8,128)S(1)}, u32[]{:S(2)}, u32[]{:S(2)}) async-start(f32[32,32,128]{2,1,0:T(8,128)} %stack.109), calls=%async_computation.1 | async-start | bytes 1048576 | tf_op jit(solution)/shard_map/all_to_all | solution.py:34
  261.9 5.1 collective-permute-done.13
  269.2 4.8 collective-permute-start.15
  278.8 4.9 collective-permute-start.16
  285.9 4.0 collective-permute-done.17
  289.9 31.9 %reduce-scatter.7.cloned.1.call-done = f32[128,128]{1,0:T(8,128)} async-done(((f32[1024,128]{1,0:T(8,128)}), f32[128,128]{1,0:T(8,128)}) %reduce-scatter.7.cloned.1.call-update) | async-done | bytes 65552 | tf_op jit(solution)/shard_map/reduce_scatter | solution.py:32
  323.4 3.5 all-to-all-start.1
  327.9 3.8 collective-permute-start.18
  337.8 10.2 %collective-permute-done.19 = f32[2,2,192,32]{3,2,1,0:T(8,128)S(1)} collective-permute-done((f32[2,2,192,32]{3,2,1,0:T(8,128)S(1)}, f32[2,2,192,32]{3,2,1,0:T(8,128)S(1)}, u32[]{:S(2)}, u32[]{:S(2)}) %collective-permute-start.19) | collective-permute-done | bytes 98336 | tf_op jit(solution)/shard_map/ppermute | solution.py:48
  387.3 114.9 %reduce-scatter.9.cloned.1.call-done = f32[32,128]{1,0:T(8,128)} async-done(((f32[1024,128]{1,0:T(8,128)}), f32[32,128]{1,0:T(8,128)}) %reduce-scatter.9.cloned.1.call-update) | async-done | bytes 16400 | tf_op jit(solution)/shard_map/reduce_scatter | solution.py:32
  503.8 7.5 %all-to-all-start.2 = ((f32[32,32,128]{2,1,0:T(8,128)}), f32[32,32,128]{2,1,0:T(8,128)S(1)}, u32[]{:S(2)}, u32[]{:S(2)}) async-start(f32[32,32,128]{2,1,0:T(8,128)} %stack.250), calls=%async_computation.5 | async-start | bytes 1048576 | tf_op jit(solution)/shard_map/all_to_all | solution.py:34
  511.5 3.1 dynamic_update_slice.11
  516.6 12.4 %all-to-all-done.2 = f32[32,32,128]{2,1,0:T(8,128)S(1)} async-done(((f32[32,32,128]{2,1,0:T(8,128)}), f32[32,32,128]{2,1,0:T(8,128)S(1)}, u32[]{:S(2)}, u32[]{:S(2)}) %all-to-all-start.2) | async-done | bytes 524320 | tf_op jit(solution)/shard_map/all_to_all | solution.py:34
  531.8 5.8 collective-permute-done.21
  539.2 5.5 collective-permute-start.23
  544.7 8.3 %collective-permute-done.22 = f32[2,2,128,32]{3,2,1,0:T(8,128)S(1)} collective-permute-done((f32[2,2,128,32]{3,2,1,0:T(8,128)S(1)}, f32[2,2,128,32]{3,2,1,0:T(8,128)S(1)}, u32[]{:S(2)}, u32[]{:S(2)}) %collective-permute-start.22) | collective-permute-done | bytes 65568 | tf_op jit(solution)/shard_map/ppermute | solution.py:19
  554.4 14.1 %reduce-scatter.11.cloned.1.call-done = f32[128,128]{1,0:T(8,128)} async-done(((f32[1024,128]{1,0:T(8,128)}), f32[128,128]{1,0:T(8,128)}) %reduce-scatter.11.cloned.1.call-update) | async-done | bytes 65552 | tf_op jit(solution)/shard_map/reduce_scatter | solution.py:32
  570.1 3.5 all-to-all-start.3
  574.9 7.4 %all-to-all-done.3 = f32[8,128,128]{2,1,0:T(8,128)S(1)} async-done(((f32[8,128,128]{2,1,0:T(8,128)}), f32[8,128,128]{2,1,0:T(8,128)S(1)}, u32[]{:S(2)}, u32[]{:S(2)}) %all-to-all-start.3) | async-done | bytes 524320 | tf_op jit(solution)/shard_map/all_to_all | solution.py:34
  (275 shorter events, 173.9 us)
Async XLA Ops:
  7.2 239.4 %reduce-scatter.5.cloned.1.call-start = ((), (), s32[]{:S(2)}) async-start(), calls=%async_computation.8 | async-start | bytes 540672 | tf_op jit(solution)/shard_map/reduce_scatter | solution.py:32
  8.1 8.2 %collective-permute-start = (f32[2,2,32,128]{3,2,1,0:T(8,128)S(1)}, f32[2,2,32,128]{3,2,1,0:T(8,128)S(1)}, u32[]{:S(2)}, u32[]{:S(2)}) collective-permute-start(f32[2,2,32,128]{3,2,1,0:T(8,128)S(1)} %get-tuple-element.209), channel_id=1, source_target_pairs={{0,8},{8,16},{16,24},{24,32},{32,40},{40,48},{48,56},{56,64},{64,7... | collective-permute-start | bytes 196616 | tf_op jit(solution)/shard_map/ppermute | solution.py:46
  10.1 7.0 %collective-permute-start.1 = (f32[2,2,32,128]{3,2,1,0:T(8,128)S(1)}, f32[2,2,32,128]{3,2,1,0:T(8,128)S(1)}, u32[]{:S(2)}, u32[]{:S(2)}) collective-permute-start(f32[2,2,32,128]{3,2,1,0:T(8,128)S(1)} %get-tuple-element.208), channel_id=1, source_target_pairs={{8,0},{16,8},{24,16},{32,24},{40,32},{48,40},{56,48},{64,56},{72,6... | collective-permute-start | bytes 196616 | tf_op jit(solution)/shard_map/ppermute | solution.py:48
  17.3 9.8 %collective-permute-start.2 = (f32[2,2,192,32]{3,2,1,0:T(8,128)S(1)}, f32[2,2,192,32]{3,2,1,0:T(8,128)S(1)}, u32[]{:S(2)}, u32[]{:S(2)}) collective-permute-start(f32[2,2,192,32]{3,2,1,0:T(8,128)S(1)} %get-tuple-element.191), channel_id=1, source_target_pairs={{0,1},{1,2},{2,3},{3,4},{4,5},{5,6},{6,7},{8,9},{9,10},{10,11},{11... | collective-permute-start | bytes 294920 | tf_op jit(solution)/shard_map/ppermute | solution.py:46
  20.4 18.2 %collective-permute-start.3 = (f32[2,2,192,32]{3,2,1,0:T(8,128)S(1)}, f32[2,2,192,32]{3,2,1,0:T(8,128)S(1)}, u32[]{:S(2)}, u32[]{:S(2)}) collective-permute-start(f32[2,2,192,32]{3,2,1,0:T(8,128)S(1)} %get-tuple-element.190), channel_id=1, source_target_pairs={{1,0},{2,1},{3,2},{4,3},{5,4},{6,5},{7,6},{9,8},{10,9},{11,10},{12... | collective-permute-start | bytes 294920 | tf_op jit(solution)/shard_map/ppermute | solution.py:48
  81.1 5.6 collective-permute-start.4
  83.7 9.2 %collective-permute-start.5 = (f32[2,2,32,192]{3,2,1,0:T(8,128)S(1)}, f32[2,2,32,192]{3,2,1,0:T(8,128)S(1)}, u32[]{:S(2)}, u32[]{:S(2)}) collective-permute-start(f32[2,2,32,192]{3,2,1,0:T(8,128)S(1)} %get-tuple-element.166), channel_id=1, source_target_pairs={{0,8},{8,16},{16,24},{24,32},{32,40},{40,48},{48,56},{56,64},{64,7... | collective-permute-start | bytes 294920 | tf_op jit(solution)/shard_map/ppermute | solution.py:19
  93.0 11.2 %collective-permute-start.6 = (f32[2,2,128,32]{3,2,1,0:T(8,128)S(1)}, f32[2,2,128,32]{3,2,1,0:T(8,128)S(1)}, u32[]{:S(2)}, u32[]{:S(2)}) collective-permute-start(f32[2,2,128,32]{3,2,1,0:T(8,128)S(1)} %get-tuple-element.185), channel_id=1, source_target_pairs={{1,0},{2,1},{3,2},{4,3},{5,4},{6,5},{7,6},{9,8},{10,9},{11,10},{12... | collective-permute-start | bytes 196616 | tf_op jit(solution)/shard_map/ppermute | solution.py:19
  94.5 11.0 %collective-permute-start.7 = (f32[2,2,128,32]{3,2,1,0:T(8,128)S(1)}, f32[2,2,128,32]{3,2,1,0:T(8,128)S(1)}, u32[]{:S(2)}, u32[]{:S(2)}) collective-permute-start(f32[2,2,128,32]{3,2,1,0:T(8,128)S(1)} %get-tuple-element.184), channel_id=1, source_target_pairs={{0,1},{1,2},{2,3},{3,4},{4,5},{5,6},{6,7},{8,9},{9,10},{10,11},{11... | collective-permute-start | bytes 196616 | tf_op jit(solution)/shard_map/ppermute | solution.py:19
  106.1 11.0 %collective-permute-start.8 = (f32[2,2,32,128]{3,2,1,0:T(8,128)S(1)}, f32[2,2,32,128]{3,2,1,0:T(8,128)S(1)}, u32[]{:S(2)}, u32[]{:S(2)}) collective-permute-start(f32[2,2,32,128]{3,2,1,0:T(8,128)S(1)} %get-tuple-element.202), channel_id=1, source_target_pairs={{0,8},{8,16},{16,24},{24,32},{32,40},{40,48},{48,56},{56,64},{64,7... | collective-permute-start | bytes 196616 | tf_op jit(solution)/shard_map/ppermute | solution.py:46
  108.0 9.0 %collective-permute-start.9 = (f32[2,2,32,128]{3,2,1,0:T(8,128)S(1)}, f32[2,2,32,128]{3,2,1,0:T(8,128)S(1)}, u32[]{:S(2)}, u32[]{:S(2)}) collective-permute-start(f32[2,2,32,128]{3,2,1,0:T(8,128)S(1)} %get-tuple-element.203), channel_id=1, source_target_pairs={{8,0},{16,8},{24,16},{32,24},{40,32},{48,40},{56,48},{64,56},{72,6... | collective-permute-start | bytes 196616 | tf_op jit(solution)/shard_map/ppermute | solution.py:48
  118.0 12.9 %collective-permute-start.10 = (f32[2,2,192,32]{3,2,1,0:T(8,128)}, f32[2,2,192,32]{3,2,1,0:T(8,128)S(1)}, u32[]{:S(2)}, u32[]{:S(2)}) collective-permute-start(f32[2,2,192,32]{3,2,1,0:T(8,128)} %get-tuple-element.189), channel_id=1, source_target_pairs={{0,1},{1,2},{2,3},{3,4},{4,5},{5,6},{6,7},{8,9},{9,10},{10,11},{11... | collective-permute-start | bytes 294920 | tf_op jit(solution)/shard_map/ppermute | solution.py:46
  122.9 20.8 %collective-permute-start.11 = (f32[2,2,192,32]{3,2,1,0:T(8,128)S(1)}, f32[2,2,192,32]{3,2,1,0:T(8,128)S(1)}, u32[]{:S(2)}, u32[]{:S(2)}) collective-permute-start(f32[2,2,192,32]{3,2,1,0:T(8,128)S(1)} %get-tuple-element.188), channel_id=1, source_target_pairs={{1,0},{2,1},{3,2},{4,3},{5,4},{6,5},{7,6},{9,8},{10,9},{11,10},{12... | collective-permute-start | bytes 294920 | tf_op jit(solution)/shard_map/ppermute | solution.py:48
  248.2 25.8 %all-to-all-start = ((f32[32,32,128]{2,1,0:T(8,128)}), f32[32,32,128]{2,1,0:T(8,128)S(1)}, u32[]{:S(2)}, u32[]{:S(2)}) async-start(f32[32,32,128]{2,1,0:T(8,128)} %stack.109), calls=%async_computation.1 | async-start | bytes 1048576 | tf_op jit(solution)/shard_map/all_to_all | solution.py:34
  255.7 66.0 %reduce-scatter.7.cloned.1.call-start = ((), (), s32[]{:S(2)}) async-start(), calls=%async_computation.9 | async-start | bytes 589824 | tf_op jit(solution)/shard_map/reduce_scatter | solution.py:32
  255.8 6.0 %collective-permute-start.12 = (f32[2,2,32,192]{3,2,1,0:T(8,128)S(1)}, f32[2,2,32,192]{3,2,1,0:T(8,128)S(1)}, u32[]{:S(2)}, u32[]{:S(2)}) collective-permute-start(f32[2,2,32,192]{3,2,1,0:T(8,128)S(1)} %get-tuple-element.165), channel_id=1, source_target_pairs={{8,0},{16,8},{24,16},{32,24},{40,32},{48,40},{56,48},{64,56},{72,6... | collective-permute-start | bytes 294920 | tf_op jit(solution)/shard_map/ppermute | solution.py:19
  257.9 9.0 %collective-permute-start.13 = (f32[2,2,32,192]{3,2,1,0:T(8,128)S(1)}, f32[2,2,32,192]{3,2,1,0:T(8,128)S(1)}, u32[]{:S(2)}, u32[]{:S(2)}) collective-permute-start(f32[2,2,32,192]{3,2,1,0:T(8,128)S(1)} %get-tuple-element.164), channel_id=1, source_target_pairs={{0,8},{8,16},{16,24},{24,32},{32,40},{40,48},{48,56},{56,64},{64,7... | collective-permute-start | bytes 294920 | tf_op jit(solution)/shard_map/ppermute | solution.py:19
  267.8 8.5 %collective-permute-start.14 = (f32[2,2,128,32]{3,2,1,0:T(8,128)S(1)}, f32[2,2,128,32]{3,2,1,0:T(8,128)S(1)}, u32[]{:S(2)}, u32[]{:S(2)}) collective-permute-start(f32[2,2,128,32]{3,2,1,0:T(8,128)S(1)} %get-tuple-element.183), channel_id=1, source_target_pairs={{1,0},{2,1},{3,2},{4,3},{5,4},{6,5},{7,6},{9,8},{10,9},{11,10},{12... | collective-permute-start | bytes 196616 | tf_op jit(solution)/shard_map/ppermute | solution.py:19
  269.2 9.0 %collective-permute-start.15 = (f32[2,2,128,32]{3,2,1,0:T(8,128)}, f32[2,2,128,32]{3,2,1,0:T(8,128)S(1)}, u32[]{:S(2)}, u32[]{:S(2)}) collective-permute-start(f32[2,2,128,32]{3,2,1,0:T(8,128)} %get-tuple-element.182), channel_id=1, source_target_pairs={{0,1},{1,2},{2,3},{3,4},{4,5},{5,6},{6,7},{8,9},{9,10},{10,11},{11... | collective-permute-start | bytes 196616 | tf_op jit(solution)/shard_map/ppermute | solution.py:19
  278.8 7.1 %collective-permute-start.16 = (f32[2,2,32,128]{3,2,1,0:T(8,128)S(1)}, f32[2,2,32,128]{3,2,1,0:T(8,128)S(1)}, u32[]{:S(2)}, u32[]{:S(2)}) collective-permute-start(f32[2,2,32,128]{3,2,1,0:T(8,128)S(1)} %get-tuple-element.196), channel_id=1, source_target_pairs={{0,8},{8,16},{16,24},{24,32},{32,40},{40,48},{48,56},{56,64},{64,7... | collective-permute-start | bytes 196616 | tf_op jit(solution)/shard_map/ppermute | solution.py:46
  283.7 6.1 %collective-permute-start.17 = (f32[2,2,32,128]{3,2,1,0:T(8,128)S(1)}, f32[2,2,32,128]{3,2,1,0:T(8,128)S(1)}, u32[]{:S(2)}, u32[]{:S(2)}) collective-permute-start(f32[2,2,32,128]{3,2,1,0:T(8,128)S(1)} %get-tuple-element.197), channel_id=1, source_target_pairs={{8,0},{16,8},{24,16},{32,24},{40,32},{48,40},{56,48},{64,56},{72,6... | collective-permute-start | bytes 196616 | tf_op jit(solution)/shard_map/ppermute | solution.py:48
  323.4 25.0 %all-to-all-start.1 = ((f32[8,128,128]{2,1,0:T(8,128)}), f32[8,128,128]{2,1,0:T(8,128)S(1)}, u32[]{:S(2)}, u32[]{:S(2)}) async-start(f32[8,128,128]{2,1,0:T(8,128)} %stack.110), calls=%async_computation.3 | async-start | bytes 1048576 | tf_op jit(solution)/shard_map/all_to_all | solution.py:34
  326.9 175.4 %reduce-scatter.9.cloned.1.call-start = ((), (), s32[]{:S(2)}) async-start(), calls=%async_computation.10 | async-start | bytes 540672 | tf_op jit(solution)/shard_map/reduce_scatter | solution.py:32
  327.9 9.9 %collective-permute-start.18 = (f32[2,2,192,32]{3,2,1,0:T(8,128)}, f32[2,2,192,32]{3,2,1,0:T(8,128)S(1)}, u32[]{:S(2)}, u32[]{:S(2)}) collective-permute-start(f32[2,2,192,32]{3,2,1,0:T(8,128)} %get-tuple-element.187), channel_id=1, source_target_pairs={{0,1},{1,2},{2,3},{3,4},{4,5},{5,6},{6,7},{8,9},{9,10},{10,11},{11... | collective-permute-start | bytes 294920 | tf_op jit(solution)/shard_map/ppermute | solution.py:46
  331.7 16.3 %collective-permute-start.19 = (f32[2,2,192,32]{3,2,1,0:T(8,128)S(1)}, f32[2,2,192,32]{3,2,1,0:T(8,128)S(1)}, u32[]{:S(2)}, u32[]{:S(2)}) collective-permute-start(f32[2,2,192,32]{3,2,1,0:T(8,128)S(1)} %get-tuple-element.186), channel_id=1, source_target_pairs={{1,0},{2,1},{3,2},{4,3},{5,4},{6,5},{7,6},{9,8},{10,9},{11,10},{12... | collective-permute-start | bytes 294920 | tf_op jit(solution)/shard_map/ppermute | solution.py:48
  503.8 25.1 %all-to-all-start.2 = ((f32[32,32,128]{2,1,0:T(8,128)}), f32[32,32,128]{2,1,0:T(8,128)S(1)}, u32[]{:S(2)}, u32[]{:S(2)}) async-start(f32[32,32,128]{2,1,0:T(8,128)} %stack.250), calls=%async_computation.5 | async-start | bytes 1048576 | tf_op jit(solution)/shard_map/all_to_all | solution.py:34
  511.3 57.1 %reduce-scatter.11.cloned.1.call-start = ((), (), s32[]{:S(2)}) async-start(), calls=%async_computation.11 | async-start | bytes 589824 | tf_op jit(solution)/shard_map/reduce_scatter | solution.py:32
  514.7 17.1 %collective-permute-start.20 = (f32[2,2,32,192]{3,2,1,0:T(8,128)S(1)}, f32[2,2,32,192]{3,2,1,0:T(8,128)S(1)}, u32[]{:S(2)}, u32[]{:S(2)}) collective-permute-start(f32[2,2,32,192]{3,2,1,0:T(8,128)S(1)} %get-tuple-element.163), channel_id=1, source_target_pairs={{8,0},{16,8},{24,16},{32,24},{40,32},{48,40},{56,48},{64,56},{72,6... | collective-permute-start | bytes 294920 | tf_op jit(solution)/shard_map/ppermute | solution.py:19
  529.9 7.8 %collective-permute-start.21 = (f32[2,2,32,192]{3,2,1,0:T(8,128)S(1)}, f32[2,2,32,192]{3,2,1,0:T(8,128)S(1)}, u32[]{:S(2)}, u32[]{:S(2)}) collective-permute-start(f32[2,2,32,192]{3,2,1,0:T(8,128)S(1)} %get-tuple-element.162), channel_id=1, source_target_pairs={{0,8},{8,16},{16,24},{24,32},{32,40},{40,48},{48,56},{56,64},{64,7... | collective-permute-start | bytes 294920 | tf_op jit(solution)/shard_map/ppermute | solution.py:19
  537.8 15.3 %collective-permute-start.22 = (f32[2,2,128,32]{3,2,1,0:T(8,128)S(1)}, f32[2,2,128,32]{3,2,1,0:T(8,128)S(1)}, u32[]{:S(2)}, u32[]{:S(2)}) collective-permute-start(f32[2,2,128,32]{3,2,1,0:T(8,128)S(1)} %get-tuple-element.179), channel_id=1, source_target_pairs={{1,0},{2,1},{3,2},{4,3},{5,4},{6,5},{7,6},{9,8},{10,9},{11,10},{12... | collective-permute-start | bytes 196616 | tf_op jit(solution)/shard_map/ppermute | solution.py:19
  539.2 34.4 %collective-permute-start.23 = (f32[2,2,128,32]{3,2,1,0:T(8,128)S(1)}, f32[2,2,128,32]{3,2,1,0:T(8,128)S(1)}, u32[]{:S(2)}, u32[]{:S(2)}) collective-permute-start(f32[2,2,128,32]{3,2,1,0:T(8,128)S(1)} %get-tuple-element.178), channel_id=1, source_target_pairs={{0,1},{1,2},{2,3},{3,4},{4,5},{5,6},{6,7},{8,9},{9,10},{10,11},{11... | collective-permute-start | bytes 196616 | tf_op jit(solution)/shard_map/ppermute | solution.py:19
  570.1 12.1 %all-to-all-start.3 = ((f32[8,128,128]{2,1,0:T(8,128)}), f32[8,128,128]{2,1,0:T(8,128)S(1)}, u32[]{:S(2)}, u32[]{:S(2)}) async-start(f32[8,128,128]{2,1,0:T(8,128)} %stack.251), calls=%async_computation.7 | async-start | bytes 1048576 | tf_op jit(solution)/shard_map/all_to_all | solution.py:34
  (6 other events, 17.2 us)
Sparse Core Ops, SparseCore 0:
  125.2 121.3 reduce-scatter.4
  275.0 46.7 reduce-scatter.6
  387.5 114.7 reduce-scatter.8
  529.9 38.4 reduce-scatter.10
